TPU v7x, 256 devices: a whole 4x4x8 slice. The times are simulated.
256 devices in a mesh: req: 32 (over y, x, core), head: 8 (over z).
Axes of the slice: x: 4, y: 4, z: 8, core: 2. Of those that a mesh axis runs over, the one named last changes fastest.
Arguments:
- tokens: bfloat16 [4096, 1536], P(('req', 'head')), may hold values from -6 to 6
- pre_gain: float32 [1536], replicated, may hold values from 0.1 to 1.9
- inner_weight: bfloat16 [1536, 2, 3072], P(None, None, 'head')
- shared_weight: bfloat16 [1536, 304], replicated, may hold values from -0.15625 to 0.15625
- conv_inner: float32 [4, 3072], P(None, 'head'), may hold values from -0.5 to 0.5
- conv_inner_bias: float32 [3072], P('head'), may hold values from -0.5 to 0.5
- conv_shared: float32 [4, 256], replicated, may hold values from -0.5 to 0.5
- conv_shared_bias: float32 [256], replicated, may hold values from -0.5 to 0.5
- step_bias: float32 [48], P('head'), may hold values from -4 to 0
- decay_log: float32 [48], P('head'), may hold values from 0 to 2.77
- skip_gain: float32 [48], P('head'), may hold values from 0.5 to 1.5
- gate_gain: float32 [3072], P('head'), may hold values from 0.1 to 1.9
- out_weight: bfloat16 [3072, 1536], P('head'), may hold values from -0.109375 to 0.109375
- states: bfloat16 [1024, 48, 64, 128], P('req', 'head'), may hold values from -1.1953125 to 1.1953125
- edge_inner: bfloat16 [1024, 3, 3072], P('req', None, 'head'), may hold values from -6 to 6
- edge_shared: bfloat16 [1024, 3, 256], P('req'), may hold values from -6 to 6
- counts: int32 [1024], P('req'), may hold values from 1 to 4, as said below
- mig_ids: int32 [32], replicated, may hold values from 0 to 1023, as said below
- mig_dest: int32 [32], replicated, may hold values from 0 to 1023, as said below
- reorder: int32 [1024], replicated, may hold values from 0 to 1023, as said below
Outputs:
- hidden_out: bfloat16 [4096, 1536], P(('req', 'head'))
- states_out: bfloat16 [1024, 48, 64, 128], P('req', 'head')
- edge_inner_out: bfloat16 [1024, 3, 3072], P('req', None, 'head')
- edge_shared_out: bfloat16 [1024, 3, 256], P('req')
Inputs may be any that keep to these rules, and one draw needn't show every extreme that they name: counts: each slot's token rows are r * 4 to r * 4 + 3 of tokens; the first counts[r] of them are real. mig_ids: distinct old slots listed by owner: entry i is one of the slots i * 32 to (i + 1) * 32 - 1, those held by index i of req. mig_dest: a reordering of the slots in mig_ids. reorder: a permutation of all slots. The 32 new slots j with j // 32 = d take at most 1 values reorder[j] of any one block of 32 slots, and exactly 1 of some block.
All inputs are finite; a program needn't handle non-finite values.
Results may differ from a plain program's by a relative error of at most 0.013.
Values may be sent and summed in bfloat16 or wider, within the bound.
A program may use at most 128 MiB of HBM per device.

v0:
```python
import jax
import jax.numpy as jnp
from jax import lax
from jax.sharding import PartitionSpec as P

EPS = 1e-05
HIGH = lax.Precision.HIGHEST


def depthwise(edge, fresh, weight, offset_bias):
    sequence = jnp.concatenate([edge, fresh], axis=1).astype(jnp.float32)
    window = fresh.shape[1]
    summed = sequence[:, 0:window] * weight[0]
    for offset in range(1, weight.shape[0]):
        summed = summed + sequence[:, offset : offset + window] * weight[offset]
    return jax.nn.silu(summed + offset_bias)


def new_edge(edge, fresh, counts):
    sequence = jnp.concatenate([edge, fresh], axis=1)
    keep_rows = edge.shape[1]
    result = edge
    for length in range(1, fresh.shape[1] + 1):
        result = jnp.where(
            (counts == length)[:, None, None], sequence[:, length : length + keep_rows], result
        )
    return result


def rank_rows(partner, position, capacity):
    matching = partner[:, None] == partner[None, :]
    earlier = position[None, :] < position[:, None]
    ranking = jnp.sum(jnp.logical_and(matching, earlier), axis=1)
    return partner * capacity + ranking


def route_rows(anchor, first_slot, slot_count, all_slots, capacity):
    inverse = jnp.zeros(all_slots.shape, jnp.int32).at[anchor].set(all_slots)
    targets = lax.dynamic_slice_in_dim(inverse, first_slot, slot_count)
    send_rows = rank_rows(targets // slot_count, targets % slot_count, capacity)
    sources = lax.dynamic_slice_in_dim(anchor, first_slot, slot_count)
    recv_rows = rank_rows(sources // slot_count, jnp.arange(slot_count, dtype=jnp.int32), capacity)
    return (send_rows, recv_rows)


def migrate(item, mig_dest, slot_count, groups, device):
    length = item.shape[0]
    piece = -(-length // groups)
    padded = jnp.pad(item, (0, piece * groups - length)).reshape(groups, piece)
    first = lax.all_to_all(padded, "req", 0, 0, tiled=True)
    dest_dev = mig_dest // slot_count
    order = jnp.zeros((groups,), jnp.int32).at[dest_dev].set(jnp.arange(groups, dtype=jnp.int32))
    second = lax.all_to_all(first[order], "req", 0, 0, tiled=True)
    arrived = second.reshape(-1)[:length]
    target_local = mig_dest[order[device]] - device * slot_count
    return (arrived, target_local)


def local(
    tokens,
    pre_gain,
    inner_weight,
    shared_weight,
    conv_inner,
    conv_inner_bias,
    conv_shared,
    conv_shared_bias,
    step_bias,
    decay_log,
    skip_gain,
    gate_gain,
    out_weight,
    states,
    edge_inner,
    edge_shared,
    counts,
    mig_ids,
    mig_dest,
    reorder,
):
    slot_count, heads_here, head_dim, state_dim = states.shape
    inner_here = heads_here * head_dim
    lanes = state_dim
    groups = lax.axis_size("req")
    device = lax.axis_index("req")
    first_slot = device * slot_count
    stride = (slot_count + groups - 1) // groups
    all_slots = jnp.arange(slot_count * groups, dtype=jnp.int32)
    rows_in = tokens.astype(jnp.float32)
    normed = (
        rows_in * lax.rsqrt(jnp.mean(rows_in * rows_in, axis=-1, keepdims=True) + EPS) * pre_gain
    ).astype(jnp.bfloat16)
    inner_flat = inner_weight.reshape(inner_weight.shape[0], 2 * inner_here)
    piece_rows = lax.all_gather(normed, "head", axis=0, tiled=True)
    inner_rows = jnp.dot(piece_rows, inner_flat, preferred_element_type=jnp.float32).astype(
        jnp.bfloat16
    )
    shared_rows = jnp.dot(piece_rows, shared_weight, preferred_element_type=jnp.float32).astype(
        jnp.bfloat16
    )
    state_rows = heads_here * head_dim * state_dim // lanes
    inner_edge_rows = edge_inner.shape[1] * edge_inner.shape[2] // lanes
    shared_edge_rows = edge_shared.shape[1] * edge_shared.shape[2] // lanes
    packed = jnp.concatenate(
        [
            states.reshape(slot_count, state_rows, lanes),
            edge_inner.reshape(slot_count, inner_edge_rows, lanes),
            edge_shared.reshape(slot_count, shared_edge_rows, lanes),
        ],
        axis=1,
    )
    row_total = packed.shape[1]
    moving = mig_ids.shape[0] // groups
    own_id = mig_ids[device * moving]
    mig_local = own_id - first_slot
    item = lax.dynamic_index_in_dim(packed, mig_local, 0, keepdims=False).reshape(-1)
    arrived, target_local = migrate(item, mig_dest, slot_count, groups, device)
    arrived = arrived.reshape(row_total, lanes)
    send_rows, recv_rows = route_rows(reorder, first_slot, slot_count, all_slots, stride)
    buffer_rows = groups * stride
    send_idx = (
        jnp.zeros((buffer_rows,), jnp.int32)
        .at[send_rows]
        .set(jnp.arange(slot_count, dtype=jnp.int32))
    )
    send_buf = jnp.where((send_idx == target_local)[:, None, None], arrived[None], packed[send_idx])
    received = lax.all_to_all(send_buf, "req", 0, 0, tiled=True)
    moved = received[recv_rows]
    moved_states = moved[:, :state_rows].reshape(slot_count, heads_here, head_dim, state_dim)
    moved_inner = moved[:, state_rows : state_rows + inner_edge_rows].reshape(edge_inner.shape)
    moved_shared = moved[:, state_rows + inner_edge_rows :].reshape(edge_shared.shape)
    window = inner_rows.shape[0] // slot_count
    inner_rows = inner_rows.reshape(slot_count, window, 2 * inner_here)
    shared_rows = shared_rows.reshape(slot_count, window, shared_rows.shape[1])
    gate_part = inner_rows[:, :, :inner_here]
    value_part = inner_rows[:, :, inner_here:]
    fresh_shared = shared_rows[:, :, : 2 * state_dim]
    head_index = lax.axis_index("head")
    step_raw = lax.dynamic_slice_in_dim(
        shared_rows[:, :, 2 * state_dim :], head_index * heads_here, heads_here, axis=2
    )
    edge_inner_out = new_edge(moved_inner, value_part, counts)
    edge_shared_out = new_edge(moved_shared, fresh_shared, counts)
    mixed_inner = depthwise(moved_inner, value_part, conv_inner, conv_inner_bias)
    mixed_shared = depthwise(moved_shared, fresh_shared, conv_shared, conv_shared_bias)
    valid = jnp.arange(window)[None, :] < counts[:, None]
    step_size = jax.nn.softplus(step_raw.astype(jnp.float32) + step_bias)
    step_size = jnp.where(valid[:, :, None], step_size, 0.0)
    decay = -jnp.exp(decay_log)
    inputs = mixed_inner.reshape(slot_count, window, heads_here, head_dim)
    entries = mixed_shared[:, :, :state_dim]
    readouts = mixed_shared[:, :, state_dim:]
    factor = jnp.exp(step_size * decay)
    cum = [factor[:, 0]]
    for t in range(1, window):
        cum.append(cum[-1] * factor[:, t])
    cumulative = jnp.stack(cum, axis=1)
    span = {}
    for t in range(window):
        span[t, t] = jnp.ones_like(factor[:, 0])
        for s in range(t - 1, -1, -1):
            span[t, s] = span[t, s + 1] * factor[:, s + 1]
    held = moved_states.astype(jnp.float32)
    from_state = jnp.einsum("rhpn,rtn->rthp", held, readouts, precision=HIGH)
    overlap = jnp.einsum("rtn,rsn->rts", readouts, entries, precision=HIGH)
    weighted = step_size[:, :, :, None] * inputs
    produced = []
    for t in range(window):
        acc = cumulative[:, t, :, None] * from_state[:, t]
        for s in range(t + 1):
            coef = span[t, s] * overlap[:, t, s, None]
            acc = acc + coef[:, :, None] * weighted[:, s]
        produced.append(acc + skip_gain[None, :, None] * inputs[:, t])
    outputs = jnp.stack(produced, axis=1)
    last = window - 1
    pushed = jnp.stack([span[last, s] for s in range(window)], axis=1)[:, :, :, None] * weighted
    update = jnp.einsum("rshp,rsn->rhpn", pushed, entries, precision=HIGH)
    final = cumulative[:, last, :, None, None] * held + update
    states_out = final.astype(jnp.bfloat16)
    outputs = outputs.reshape(slot_count, window, inner_here)
    gated = outputs * jax.nn.silu(gate_part.astype(jnp.float32))
    square_part = jnp.sum(gated * gated, axis=-1).reshape(slot_count * window, 1)
    pre_scaled = (
        jnp.where(valid[:, :, None], gated * gate_gain, 0.0)
        .astype(jnp.bfloat16)
        .reshape(slot_count * window, inner_here)
    )
    partial = jnp.dot(pre_scaled, out_weight, preferred_element_type=jnp.float32)
    extra = jnp.broadcast_to(square_part, (partial.shape[0], 128))
    combined = jnp.concatenate([partial, extra], axis=1)
    reduced = lax.psum_scatter(combined, "head", scatter_dimension=0, tiled=True)
    full_inner = inner_here * lax.axis_size("head")
    scale = lax.rsqrt(reduced[:, -1:] / full_inner + EPS)
    hidden_out = (rows_in + reduced[:, : partial.shape[1]] * scale).astype(jnp.bfloat16)
    return (hidden_out, states_out, edge_inner_out, edge_shared_out)


def solution(mesh):
    placed = (
        P(("req", "head"), None),
        P(),
        P(None, None, "head"),
        P(),
        P(None, "head"),
        P("head"),
        P(),
        P(),
        P("head"),
        P("head"),
        P("head"),
        P("head"),
        P("head", None),
        P("req", "head", None, None),
        P("req", None, "head"),
        P("req", None, None),
        P("req"),
        P(),
        P(),
        P(),
    )
    return jax.shard_map(
        local,
        mesh=mesh,
        in_specs=placed,
        out_specs=(
            P(("req", "head"), None),
            P("req", "head", None, None),
            P("req", None, "head"),
            P("req", None, None),
        ),
        check_vma=False,
    )
```

profile of v0, /device:TPU:6, one launch (start us, length us, event | category | flops | bytes accessed | tf_op | source)
XLA Modules:
  0.0 188.7 jit_solution(13441082247929192009)
XLA Ops:
  7.2 1.3 dynamic_slice.26
  9.2 0.8 copy.235
  10.1 0.9 copy.234
  11.1 2.3 %pad_maximum_fusion = bf16[32,399,128]{2,1,0:T(8,128)(2,1)S(1)} fusion(bf16[32,6,128]{2,1,0:T(8,128)(2,1)S(1)} %reshape.332, bf16[32,9,128]{2,1,0:T(8,128)(2,1)S(1)} %reshape.331, bf16[32,384,128]{2,1,0:T(8,128)(2,1)} %bitcast.73), kind=kLoop, calls=%fused_computation.7 | loop fusion | flops 9805824 | bytes 6537216 | tf_op jit(solution)/shard_map/concatenate | solution.py:104
  13.4 1.7 copy-done.1
  15.8 1.3 reduce.39
  17.1 0.8 reshape.423
  17.9 7.6 %all-to-all-start = ((bf16[32,2,798]{2,1,0:T(2,128)(2,1)}), bf16[32,2,798]{2,1,0:T(2,128)(2,1)S(1)}, u32[]{:S(2)}, u32[]{:S(2)}) async-start(bf16[32,2,798]{2,1,0:T(2,128)(2,1)} %reshape.423), calls=%async_computation | async-start | bytes 229376 | tf_op jit(solution)/shard_map/all_to_all | solution.py:50
  25.5 4.3 %scatter_custom_fusion = s32[1024]{0:T(1024)S(1)} fusion(s32[1024]{0:T(1024)S(1)} %compare_select_fusion.1, s32[1024]{0:T(1024)S(1)} %iota.23, s32[]{:T(128)} %constant.75.clone.1), kind=kCustom, calls=%fused_computation.145 | custom fusion | bytes 4100 | tf_op jit(solution)/shard_map/scatter | solution.py:38
  37.1 0.8 reshape.425
  37.9 7.4 %all-to-all-start.1 = ((bf16[32,2,798]{2,1,0:T(2,128)(2,1)}), bf16[32,2,798]{2,1,0:T(2,128)(2,1)S(1)}, u32[]{:S(2)}, u32[]{:S(2)}) async-start(bf16[32,2,798]{2,1,0:T(2,128)(2,1)} %reshape.425), calls=%async_computation.1 | async-start | bytes 229376 | tf_op jit(solution)/shard_map/all_to_all | solution.py:53
  45.3 4.6 %gather_fusion.1 = bf16[32,399,128]{2,1,0:T(8,128)(2,1)} fusion(bf16[32,399,128]{2,1,0:T(8,128)(2,1)} %copy-done.1, s32[1024]{0:T(1024)S(1)} %pad_clamp_fusion.1), kind=kCustom, calls=%fused_computation.1 | custom fusion | bytes 6537344 | tf_op jit(solution)/shard_map/gather | solution.py:126
  49.9 1.3 all-to-all-done.1
  52.3 3.9 %broadcast_select_fusion = bf16[32,399,128]{2,1,0:T(8,128)(2,1)} fusion(bf16[32,399,128]{2,1,0:T(8,128)(2,1)} %gather_fusion.1, pred[32]{0:T(512)(128)(4,1)S(1)} %broadcast_compare_fusion.3, bf16[399,128]{1,0:T(8,128)(2,1)S(1)} %broadcast_in_dim.162), kind=kLoop, calls=%fused_computation.8 | loop fusion | flops 1634304 | bytes 6639392 | tf_op jit(solution)/shard_map/jit(_where)/select_n | solution.py:126
  56.2 6.5 %all-to-all-start.2 = ((bf16[32,399,128]{2,1,0:T(8,128)(2,1)}), bf16[32,399,128]{2,1,0:T(8,128)(2,1)}, u32[]{:S(2)}, u32[]{:S(2)}) async-start(bf16[32,399,128]{2,1,0:T(8,128)(2,1)} %broadcast_select_fusion), calls=%async_computation.2 | async-start | bytes 6553600 | tf_op jit(solution)/shard_map/all_to_all | solution.py:127
  62.9 28.9 %all_gather.3 = bf16[128,1536]{1,0:T(8,128)(2,1)S(1)} all-gather(bf16[16,1536]{1,0:T(8,128)(2,1)S(1)} %fusion.17), channel_id=1, replica_groups=mesh['req'=32,'head'=8] {'head'}, dimensions={0}, use_global_device_ids=true | all-gather | bytes 442368 | tf_op jit(solution)/shard_map/all_gather | solution.py:94
  92.5 2.2 %copy.278 = bf16[192,8,2,384]{3,1,2,0:T(8,128)(2,1)S(1)} copy(bf16[192,8,2,384]{3,2,1,0:T(2,128)(2,1)} %bitcast.74) | data formatting | bytes 4718592
  95.5 0.8 copy.238
  98.8 3.4 %all-to-all-done.2 = bf16[32,399,128]{2,1,0:T(8,128)(2,1)} async-done(((bf16[32,399,128]{2,1,0:T(8,128)(2,1)}), bf16[32,399,128]{2,1,0:T(8,128)(2,1)}, u32[]{:S(2)}, u32[]{:S(2)}) %all-to-all-start.2) | async-done | bytes 3268640 | tf_op jit(solution)/shard_map/all_to_all | solution.py:127
  102.2 4.6 %gather_fusion.2 = bf16[32,399,128]{2,1,0:T(8,128)(2,1)} fusion(bf16[32,399,128]{2,1,0:T(8,128)(2,1)} %all-to-all-done.2, s32[1024]{0:T(1024)S(1)} %pad_clamp_fusion), kind=kCustom, calls=%fused_computation.2 | custom fusion | bytes 6537344 | tf_op jit(solution)/shard_map/gather | solution.py:128
  106.8 4.0 %slice.275 = bf16[32,384,128]{2,1,0:T(8,128)(2,1)} slice(bf16[32,399,128]{2,1,0:T(8,128)(2,1)} %gather_fusion.2), slice={[0:32], [0:384], [0:128]} | slice | bytes 6291456 | tf_op jit(solution)/shard_map/slice | solution.py:129
  112.0 9.3 %fusion.45 = f32[32,4,6,64]{3,1,2,0:T(4,128)S(1)} fusion(bf16[32,6,64,128]{3,2,1,0:T(8,128)(2,1)} %bitcast.69, f32[32,4,256]{2,1,0:T(4,128)S(1)} %divide_multiply_fusion.1), kind=kOutput, calls=%fused_computation.93 | convolution fusion | flops 75497472 | bytes 3407872 | tf_op jit(solution)/shard_map/rhpn,rtn->rthp/dot_general | solution.py:164
  121.3 1.6 slice_reduce_fusion.9
  126.3 1.3 broadcast_multiply_fusion
  127.5 2.9 %fusion.32 = (f32[32,6,64]{2,1,0:T(8,128)S(1)}, f32[32,6,64]{2,1,0:T(8,128)S(1)}) fusion(f32[32,4,6,64]{3,1,2,0:T(4,128)S(1)} %get-tuple-element.62, f32[32,4,6,64]{3,1,2,0:T(4,128)S(1)} %fusion.45, f32[32]{0:T(128)} %get-tuple-element.40, f32[32,6]{1,0:T(8,128)} %bitcast.76, f32[6]{0:T(128)} %param.30, f32[32,4,6,64]{3,1,2,0:T(4,128)S(1)} %get-tuple-element.61, ...), kind=kLoop, calls=%fused_computation.79 | loop fusion | flops 196608 | bytes 495640 | tf_op jit(solution)/shard_map/add | solution.py:173
  133.6 2.4 %fusion.31 = (f32[32,6,64]{2,1,0:T(8,128)S(1)}, f32[32,6,64]{2,1,0:T(8,128)S(1)}) fusion(f32[32,4,6,64]{3,1,2,0:T(4,128)S(1)} %get-tuple-element.62, f32[32,4,6,64]{3,1,2,0:T(4,128)S(1)} %fusion.45, f32[32]{0:T(128)} %get-tuple-element.48, f32[32,6]{1,0:T(8,128)S(1)} %copy.244, f32[32,6]{1,0:T(8,128)S(1)} %copy.243, f32[6]{0:T(128)} %param.30, ...), kind=kLoop, calls=%fused_computation.78 | loop fusion | flops 196608 | bytes 446488 | tf_op jit(solution)/shard_map/add | solution.py:173
  136.3 1.0 select_convert_fusion
  138.2 1.0 pad_maximum_fusion.1
  141.2 13.4 %add_convert_fusion = bf16[32,6,64,128]{3,2,1,0:T(8,128)(2,1)} fusion(bf16[32,6,64,128]{3,2,1,0:T(8,128)(2,1)} %bitcast.70, f32[32,6]{1,0:T(8,128)S(1)} %copy-done.10, f32[32,4,6,64]{3,1,2,0:T(4,128)S(1)} %get-tuple-element.61, f32[32,4,6]{1,2,0:T(8,128)S(1)} %copy.259, f32[32,4,256]{2,1,0:T(4,128)S(1)} %divide_multiply_fusion.1), kind=kOutput, calls=%fused_computation.6 | convolution fusion | flops 81838080 | bytes 6897664 | tf_op jit(solution)/shard_map/rshp,rsn->rhpn/dot_general | solution.py:177
  154.6 24.7 %reduce-scatter.2.cloned.1.call-done = f32[16,1664]{1,0:T(8,128)} async-done(((f32[128,1664]{1,0:T(8,128)}), f32[16,1664]{1,0:T(8,128)}) %reduce-scatter.2.cloned.1.call-update) | async-done | bytes 106512 | tf_op jit(solution)/shard_map/reduce_scatter | solution.py:191
  179.3 0.9 fusion.56
  180.2 1.6 fusion.18
  (147 shorter events, 21.2 us)
Async XLA Ops:
  7.2 130.6 %copy-start = (bf16[384,1536]{1,0:T(8,128)(2,1)S(1)}, bf16[384,1536]{1,0:T(8,128)(2,1)}, u32[]{:S(2)}) copy-start(bf16[384,1536]{1,0:T(8,128)(2,1)} %param.32) | copy-start | bytes 3538948
  11.1 14.4 %copy-start.15 = (s32[1024]{0:T(1024)S(1)}, s32[1024]{0:T(1024)}, u32[]{:S(2)}) copy-start(s32[1024]{0:T(1024)} %param.39) | copy-start | bytes 12292
  11.1 19.8 %copy-start.23 = (s32[32]{0:T(128)S(1)}, s32[32]{0:T(128)}, u32[]{:S(2)}) copy-start(s32[32]{0:T(128)} %param.38) | copy-start | bytes 388
  11.1 22.4 %copy-start.8 = (bf16[16,1536]{1,0:T(8,128)(2,1)S(1)}, bf16[16,1536]{1,0:T(8,128)(2,1)}, u32[]{:S(2)}) copy-start(bf16[16,1536]{1,0:T(8,128)(2,1)} %param.20) | copy-start | bytes 147460
  13.4 1.7 copy-start.1
  17.9 17.7 %all-to-all-start = ((bf16[32,2,798]{2,1,0:T(2,128)(2,1)}), bf16[32,2,798]{2,1,0:T(2,128)(2,1)S(1)}, u32[]{:S(2)}, u32[]{:S(2)}) async-start(bf16[32,2,798]{2,1,0:T(2,128)(2,1)} %reshape.423), calls=%async_computation | async-start | bytes 229376 | tf_op jit(solution)/shard_map/all_to_all | solution.py:50
  37.9 13.3 %all-to-all-start.1 = ((bf16[32,2,798]{2,1,0:T(2,128)(2,1)}), bf16[32,2,798]{2,1,0:T(2,128)(2,1)S(1)}, u32[]{:S(2)}, u32[]{:S(2)}) async-start(bf16[32,2,798]{2,1,0:T(2,128)(2,1)} %reshape.425), calls=%async_computation.1 | async-start | bytes 229376 | tf_op jit(solution)/shard_map/all_to_all | solution.py:53
  56.2 6.6 %copy-start.13 = (f32[1536]{0:T(1024)S(1)}, f32[1536]{0:T(1024)}, u32[]{:S(2)}) copy-start(f32[1536]{0:T(1024)} %param.21) | copy-start | bytes 18436
  56.2 35.6 %copy-start.3 = (bf16[1536,304]{0,1:T(8,128)(2,1)S(1)}, bf16[1536,304]{0,1:T(8,128)(2,1)}, u32[]{:S(2)}) copy-start(bf16[1536,304]{0,1:T(8,128)(2,1)} %param.23) | copy-start | bytes 2801668
  56.2 45.9 %all-to-all-start.2 = ((bf16[32,399,128]{2,1,0:T(8,128)(2,1)}), bf16[32,399,128]{2,1,0:T(8,128)(2,1)}, u32[]{:S(2)}, u32[]{:S(2)}) async-start(bf16[32,399,128]{2,1,0:T(8,128)(2,1)} %broadcast_select_fusion), calls=%async_computation.2 | async-start | bytes 6553600 | tf_op jit(solution)/shard_map/all_to_all | solution.py:127
  62.7 116.6 %reduce-scatter.2.cloned.1.call-start = ((), (), s32[]{:S(2)}) async-start(), calls=%async_computation.4 | async-start | bytes 958464 | tf_op jit(solution)/shard_map/reduce_scatter | solution.py:191
  92.4 3.0 %copy-start.21 = (s32[32]{0:T(128)S(1)}, s32[32]{0:T(128)}, u32[]{:S(2)}) copy-start(s32[32]{0:T(128)} %param.36) | copy-start | bytes 388
  92.4 3.0 %copy-start.24 = (f32[6]{0:T(128)S(1)}, f32[6]{0:T(128)}, u32[]{:S(2)}) copy-start(f32[6]{0:T(128)} %param.29) | copy-start | bytes 76
  92.4 3.0 %copy-start.20 = (f32[6]{0:T(128)S(1)}, f32[6]{0:T(128)}, u32[]{:S(2)}) copy-start(f32[6]{0:T(128)} %param.28) | copy-start | bytes 76
  92.4 5.5 %copy-start.14 = (f32[4,384]{1,0:T(4,128)S(1)}, f32[4,384]{1,0:T(4,128)}, u32[]{:S(2)}) copy-start(f32[4,384]{1,0:T(4,128)} %param.24) | copy-start | bytes 18436
  92.5 5.6 %copy-start.16 = (f32[4,256]{1,0:T(4,128)S(1)}, f32[4,256]{1,0:T(4,128)}, u32[]{:S(2)}) copy-start(f32[4,256]{1,0:T(4,128)} %param.26) | copy-start | bytes 12292
  95.4 11.4 %copy-start.18 = (pred[32,4]{0,1:T(4,128)(4,1)}, pred[32,4]{0,1:T(4,128)(4,1)S(1)}, u32[]{:S(2)}) copy-start(pred[32,4]{0,1:T(4,128)(4,1)S(1)} %iota_compare_fusion.1) | copy-start | bytes 388
  106.8 4.1 %copy-start.2 = (bf16[32,399,128]{2,1,0:T(8,128)(2,1)S(1)}, bf16[32,399,128]{2,1,0:T(8,128)(2,1)}, u32[]{:S(2)}) copy-start(bf16[32,399,128]{2,1,0:T(8,128)(2,1)} %gather_fusion.2) | copy-start | bytes 9805828
  106.8 4.1 %slice-start = ((bf16[32,399,128]{2,1,0:T(8,128)(2,1)}), bf16[32,9,128]{2,1,0:T(8,128)(2,1)S(1)}, s32[]{:S(2)}) async-start(bf16[32,399,128]{2,1,0:T(8,128)(2,1)} %gather_fusion.2), calls=%async_computation.5 | async-start | bytes 262144 | tf_op jit(solution)/shard_map/slice | solution.py:130
  106.8 4.3 %copy-start.17 = (f32[384]{0:T(512)S(1)}, f32[384]{0:T(512)}, u32[]{:S(2)}) copy-start(f32[384]{0:T(512)} %param.25) | copy-start | bytes 4612
  110.8 0.7 copy-start.19
  110.9 10.4 %copy-start.4 = (bf16[32,3,384]{2,1,0:T(4,128)(2,1)}, bf16[32,3,384]{2,1,0:T(4,128)(2,1)S(1)}, u32[]{:S(2)}) copy-start(bf16[32,3,384]{2,1,0:T(4,128)(2,1)S(1)} %reshape.335) | copy-start | bytes 221188
  111.3 14.3 %copy-start.6 = (bf16[32,3,256]{2,1,0:T(4,128)(2,1)}, bf16[32,3,256]{2,1,0:T(4,128)(2,1)S(1)}, u32[]{:S(2)}) copy-start(bf16[32,3,256]{2,1,0:T(4,128)(2,1)S(1)} %reshape.333) | copy-start | bytes 147460
  136.0 3.3 %copy-start.11 = (f32[32,1,6]{0,1,2:T(1,128)S(1)}, f32[32,1,6]{0,1,2:T(1,128)}, u32[]{:S(2)}) copy-start(f32[32,1,6]{0,1,2:T(1,128)} %get-tuple-element.54) | copy-start | bytes 2308
  136.0 3.3 %copy-start.12 = (f32[32,1,6]{0,1,2:T(1,128)S(1)}, f32[32,1,6]{0,1,2:T(1,128)}, u32[]{:S(2)}) copy-start(f32[32,1,6]{0,1,2:T(1,128)} %get-tuple-element.55) | copy-start | bytes 2308
  136.0 3.5 %copy-start.22 = (s32[32]{0:T(128)S(1)}, s32[32]{0:T(128)}, u32[]{:S(2)}) copy-start(s32[32]{0:T(128)} %param.36) | copy-start | bytes 388
  136.3 3.3 %copy-start.7 = (bf16[32,3,256]{2,1,0:T(4,128)(2,1)S(1)}, bf16[32,3,256]{2,1,0:T(4,128)(2,1)}, u32[]{:S(2)}) copy-start(bf16[32,3,256]{2,1,0:T(4,128)(2,1)} %copy-done.6) | copy-start | bytes 147460
  137.3 3.2 %copy-start.5 = (bf16[32,3,384]{2,1,0:T(4,128)(2,1)S(1)}, bf16[32,3,384]{2,1,0:T(4,128)(2,1)}, u32[]{:S(2)}) copy-start(bf16[32,3,384]{2,1,0:T(4,128)(2,1)} %copy-done.4) | copy-start | bytes 221188
  137.6 3.6 %copy-start.10 = (f32[32,6]{1,0:T(8,128)S(1)}, f32[32,6]{1,0:T(8,128)}, u32[]{:S(2)}) copy-start(f32[32,6]{1,0:T(8,128)} %copy.250) | copy-start | bytes 2308
  141.2 39.0 %copy-start.9 = (bf16[16,1536]{1,0:T(8,128)(2,1)S(1)}, bf16[16,1536]{1,0:T(8,128)(2,1)}, u32[]{:S(2)}) copy-start(bf16[16,1536]{1,0:T(8,128)(2,1)} %param.20) | copy-start | bytes 147460
Sparse Core Ops, SparseCore 0:
  139.3 39.9 reduce-scatter.1
where the time goes:
time: 190 us; the launch traced here: 189 us
  local copies, waits for them, and re-layouts  42.9 us (23%)
  waiting for transfers between devices  29.5 us (16%)
  blocking collectives  28.9 us (15%)
  matrix products  24.2 us (13%)
  other arithmetic  23.6 us (12%)
  starting transfers between devices  21.5 us (11%)
  between operations  18 us (9%)
    all_gather x1, blocking collectives, local(): piece_rows = lax.all_gather(normed, 'head', axis=0, tiled=True)  28.9 us
    reduce_scatter x1, waiting for transfers between devices, local(): lax.psum_scatter(combined, 'head', scatter_dimension=0, tiled=True)  24.7 us
    dot_general x1, matrix products, local(): update = jnp.einsum('rshp,rsn->rhpn', pushed, entries, precision=HIGH)  13.4 us
    dot_general x1, matrix products, local(): from_state = jnp.einsum('rhpn,rtn->rthp', held, readouts, precision=HIGH)  9.26 us
    unnamed x61, local copies, waits for them, and re-layouts  8.57 us
    all_to_all x1, starting transfers between devices, migrate(): first = lax.all_to_all(padded, 'req', 0, 0, tiled=True)  7.56 us
    all_to_all x1, starting transfers between devices, migrate(): second = lax.all_to_all(first[order], 'req', 0, 0, tiled=True)  7.38 us
    all_to_all x1, starting transfers between devices, local(): received = lax.all_to_all(send_buf, 'req', 0, 0, tiled=True)  6.51 us
  transfers between devices with their start and end apart: 4, of which 3 were waited for; matrix products, arithmetic and copies ran while one was open for 18% of the time, Pallas kernels for 0%

commit v1 on v0

--- a/solution.py
+++ b/solution.py
@@ -91,7 +91,9 @@
         rows_in * lax.rsqrt(jnp.mean(rows_in * rows_in, axis=-1, keepdims=True) + EPS) * pre_gain
     ).astype(jnp.bfloat16)
     inner_flat = inner_weight.reshape(inner_weight.shape[0], 2 * inner_here)
-    piece_rows = lax.all_gather(normed, "head", axis=0, tiled=True)
+    piece_rows = jnp.concatenate(
+        lax.all_to_all(jnp.stack([normed] * lax.axis_size("head")), "head", 0, 0), axis=0
+    )
     inner_rows = jnp.dot(piece_rows, inner_flat, preferred_element_type=jnp.float32).astype(
         jnp.bfloat16
     )

time: 190 us -> 202 us (1.063)
  blocking collectives: 28.9 us -> 0 us
  waiting for transfers between devices: 29.5 us -> 44.1 us
  local copies, waits for them, and re-layouts: 42.9 us -> 54 us
  starting transfers between devices: 21.5 us -> 30 us
  matrix products: 24.2 us -> 27.8 us
  other arithmetic: 23.6 us -> 26.2 us
    all_gather x1 -> x0, blocking collectives: 28.9 us -> none  [local(): piece_rows = lax.all_gather(normed, 'head', axis=0, tiled=True)]
    all_to_all x1, waiting for transfers between devices: 3.41 us -> 16.7 us  [local(): received = lax.all_to_all(send_buf, 'req', 0, 0, tiled=True)]
    all_to_all x0 -> x1, starting transfers between devices: none -> 8.47 us  [local(): lax.all_to_all(jnp.stack([normed] * lax.axis_size('head')), 'head', 0, 0)]
    reduce_scatter x1, waiting for transfers between devices: 24.7 us -> 19.9 us  [local(): lax.psum_scatter(combined, 'head', scatter_dimension=0, tiled=True)]
    all_to_all x0 -> x1, waiting for transfers between devices: none -> 3.56 us  [local(): lax.all_to_all(jnp.stack([normed] * lax.axis_size('head')), 'head', 0, 0)]
    all_to_all x1, waiting for transfers between devices: 1.33 us -> 3.97 us  [migrate(): second = lax.all_to_all(first[order], 'req', 0, 0, tiled=True)]
    unnamed x61 -> x67, local copies, waits for them, and re-layouts: 8.57 us -> 9.29 us
  transfers between devices with their start and end apart: 4 -> 5, of which waited for: 3 -> 4; matrix products, arithmetic and copies ran while one was open for 18% -> 27% of each run, Pallas kernels for 0% -> 0%
where the time goes in v1:
time: 202 us; the launch traced here: 200 us
  local copies, waits for them, and re-layouts  54 us (27%)
  waiting for transfers between devices  44.1 us (22%)
  starting transfers between devices  30 us (15%)
  matrix products  27.8 us (14%)
  other arithmetic  26.2 us (13%)
  between operations  17.9 us (9%)
    reduce_scatter x1, waiting for transfers between devices, local(): lax.psum_scatter(combined, 'head', scatter_dimension=0, tiled=True)  19.9 us
    all_to_all x1, waiting for transfers between devices, local(): received = lax.all_to_all(send_buf, 'req', 0, 0, tiled=True)  16.7 us
    dot_general x1, matrix products, local(): update = jnp.einsum('rshp,rsn->rhpn', pushed, entries, precision=HIGH)  13.4 us
    unnamed x67, local copies, waits for them, and re-layouts  9.29 us
    dot_general x1, matrix products, local(): from_state = jnp.einsum('rhpn,rtn->rthp', held, readouts, precision=HIGH)  9.26 us
    all_to_all x1, starting transfers between devices, local(): lax.all_to_all(jnp.stack([normed] * lax.axis_size('head')), 'head', 0, 0)  8.47 us
    all_to_all x1, starting transfers between devices, migrate(): first = lax.all_to_all(padded, 'req', 0, 0, tiled=True)  7.56 us
    all_to_all x1, starting transfers between devices, migrate(): second = lax.all_to_all(first[order], 'req', 0, 0, tiled=True)  7.38 us
  transfers between devices with their start and end apart: 5, of which 4 were waited for; matrix products, arithmetic and copies ran while one was open for 27% of the time, Pallas kernels for 0%

profile of v1, /device:TPU:6, one launch (start us, length us, event | category | flops | bytes accessed | tf_op | source)
XLA Modules:
  0.0 200.1 jit_solution(9827122690681241946)
XLA Ops:
  7.2 1.3 dynamic_slice.26
  11.1 2.3 %pad_maximum_fusion = bf16[32,399,128]{2,1,0:T(8,128)(2,1)S(1)} fusion(bf16[32,6,128]{2,1,0:T(8,128)(2,1)S(1)} %reshape.338, bf16[32,9,128]{2,1,0:T(8,128)(2,1)S(1)} %reshape.337, bf16[32,384,128]{2,1,0:T(8,128)(2,1)} %bitcast.76), kind=kLoop, calls=%fused_computation.7 | loop fusion | flops 9805824 | bytes 6537216 | tf_op jit(solution)/shard_map/concatenate | solution.py:106
  13.4 1.7 copy-done.1
  15.8 1.3 reduce.39
  17.9 7.6 %all-to-all-start.1 = ((bf16[32,2,798]{2,1,0:T(2,128)(2,1)}), bf16[32,2,798]{2,1,0:T(2,128)(2,1)S(1)}, u32[]{:S(2)}, u32[]{:S(2)}) async-start(bf16[32,2,798]{2,1,0:T(2,128)(2,1)} %reshape.429), calls=%async_computation.1 | async-start | bytes 229376 | tf_op jit(solution)/shard_map/all_to_all | solution.py:50
  25.7 4.3 %scatter_custom_fusion = s32[1024]{0:T(1024)S(1)} fusion(s32[1024]{0:T(1024)S(1)} %compare_select_fusion.1, s32[1024]{0:T(1024)S(1)} %iota.23, s32[]{:T(128)} %constant.75.clone.1), kind=kCustom, calls=%fused_computation.145 | custom fusion | bytes 4100 | tf_op jit(solution)/shard_map/scatter | solution.py:38
  34.2 7.4 %all-to-all-start.2 = ((bf16[32,2,798]{2,1,0:T(2,128)(2,1)}), bf16[32,2,798]{2,1,0:T(2,128)(2,1)S(1)}, u32[]{:S(2)}, u32[]{:S(2)}) async-start(bf16[32,2,798]{2,1,0:T(2,128)(2,1)} %reshape.431), calls=%async_computation.2 | async-start | bytes 229376 | tf_op jit(solution)/shard_map/all_to_all | solution.py:53
  43.5 4.0 %all-to-all-done.2 = bf16[32,2,798]{2,1,0:T(2,128)(2,1)S(1)} async-done(((bf16[32,2,798]{2,1,0:T(2,128)(2,1)}), bf16[32,2,798]{2,1,0:T(2,128)(2,1)S(1)}, u32[]{:S(2)}, u32[]{:S(2)}) %all-to-all-start.2) | async-done | bytes 102176 | tf_op jit(solution)/shard_map/all_to_all | solution.py:53
  48.3 8.5 %all-to-all-start = ((bf16[8,16,1536]{2,1,0:T(8,128)(2,1)}), bf16[8,16,1536]{2,1,0:T(8,128)(2,1)S(1)}, u32[]{:S(2)}, u32[]{:S(2)}) async-start(bf16[8,16,1536]{2,1,0:T(8,128)(2,1)} %stack.14), calls=%async_computation | async-start | bytes 786432 | tf_op jit(solution)/shard_map/all_to_all | solution.py:95
  56.8 4.6 %gather_fusion.1 = bf16[32,399,128]{2,1,0:T(8,128)(2,1)} fusion(bf16[32,399,128]{2,1,0:T(8,128)(2,1)} %copy-done.1, s32[1024]{0:T(1024)S(1)} %pad_clamp_fusion.1), kind=kCustom, calls=%fused_computation.1 | custom fusion | bytes 6537344 | tf_op jit(solution)/shard_map/gather | solution.py:128
  64.2 3.9 %broadcast_select_fusion = bf16[32,399,128]{2,1,0:T(8,128)(2,1)} fusion(bf16[32,399,128]{2,1,0:T(8,128)(2,1)} %gather_fusion.1, pred[32]{0:T(512)(128)(4,1)S(1)} %broadcast_compare_fusion.3, bf16[399,128]{1,0:T(8,128)(2,1)S(1)} %broadcast_in_dim.162), kind=kLoop, calls=%fused_computation.8 | loop fusion | flops 1634304 | bytes 6639392 | tf_op jit(solution)/shard_map/jit(_where)/select_n | solution.py:128
  68.1 3.6 %all-to-all-done = bf16[8,16,1536]{2,1,0:T(8,128)(2,1)S(1)} async-done(((bf16[8,16,1536]{2,1,0:T(8,128)(2,1)}), bf16[8,16,1536]{2,1,0:T(8,128)(2,1)S(1)}, u32[]{:S(2)}, u32[]{:S(2)}) %all-to-all-start) | async-done | bytes 393248 | tf_op jit(solution)/shard_map/all_to_all | solution.py:95
  72.4 6.4 %all-to-all-start.3 = ((bf16[32,399,128]{2,1,0:T(8,128)(2,1)}), bf16[32,399,128]{2,1,0:T(8,128)(2,1)}, u32[]{:S(2)}, u32[]{:S(2)}) async-start(bf16[32,399,128]{2,1,0:T(8,128)(2,1)} %broadcast_select_fusion), calls=%async_computation.3 | async-start | bytes 6553600 | tf_op jit(solution)/shard_map/all_to_all | solution.py:129
  79.1 2.1 %copy.278 = bf16[192,8,2,384]{3,1,2,0:T(8,128)(2,1)S(1)} copy(bf16[192,8,2,384]{3,2,1,0:T(2,128)(2,1)} %bitcast.77) | data formatting | bytes 4718592
  84.2 1.4 fusion.72
  85.6 2.3 %convolution_convert_fusion.1 = bf16[128,304]{0,1:T(8,128)(2,1)} fusion(bf16[128,1536]{1,0:T(8,128)(2,1)} %bitcast.74, bf16[1536,304]{0,1:T(8,128)(2,1)} %param.23), kind=kOutput, calls=%fused_computation.10 | convolution fusion | flops 119576576 | bytes 1404928 | tf_op jit(solution)/shard_map/dot_general | solution.py:100
  87.9 1.6 copy.230
  89.5 1.6 reshape.335
  91.1 1.4 slice.266
  92.5 1.5 slice.269
  94.0 2.1 %convolution_convert_fusion = bf16[128,768]{1,0:T(8,128)(2,1)} fusion(bf16[128,1536]{1,0:T(8,128)(2,1)} %bitcast.75, bf16[1536,768]{1,0:T(8,128)(2,1)S(1)} %bitcast.72), kind=kOutput, calls=%fused_computation.9 | convolution fusion | flops 302088192 | bytes 2949120 | tf_op jit(solution)/shard_map/dot_general | solution.py:97
  101.6 16.7 %all-to-all-done.3 = bf16[32,399,128]{2,1,0:T(8,128)(2,1)} async-done(((bf16[32,399,128]{2,1,0:T(8,128)(2,1)}), bf16[32,399,128]{2,1,0:T(8,128)(2,1)}, u32[]{:S(2)}, u32[]{:S(2)}) %all-to-all-start.3) | async-done | bytes 3268640 | tf_op jit(solution)/shard_map/all_to_all | solution.py:129
  118.3 4.7 %gather_fusion.2 = bf16[32,399,128]{2,1,0:T(8,128)(2,1)} fusion(bf16[32,399,128]{2,1,0:T(8,128)(2,1)} %all-to-all-done.3, s32[1024]{0:T(1024)} %pad_clamp_fusion), kind=kCustom, calls=%fused_computation.2 | custom fusion | bytes 6537344 | tf_op jit(solution)/shard_map/gather | solution.py:130
  123.0 4.0 %slice.275 = bf16[32,384,128]{2,1,0:T(8,128)(2,1)} slice(bf16[32,399,128]{2,1,0:T(8,128)(2,1)} %gather_fusion.2), slice={[0:32], [0:384], [0:128]} | slice | bytes 6291456 | tf_op jit(solution)/shard_map/slice | solution.py:131
  128.3 9.3 %fusion.45 = f32[32,4,6,64]{3,1,2,0:T(4,128)S(1)} fusion(bf16[32,6,64,128]{3,2,1,0:T(8,128)(2,1)} %bitcast.70, f32[32,4,256]{2,1,0:T(4,128)S(1)} %divide_multiply_fusion.1), kind=kOutput, calls=%fused_computation.93 | convolution fusion | flops 75497472 | bytes 3407872 | tf_op jit(solution)/shard_map/rhpn,rtn->rthp/dot_general | solution.py:166
  137.6 1.6 slice_reduce_fusion.9
  142.5 1.3 broadcast_multiply_fusion
  143.8 2.9 %fusion.32 = (f32[32,6,64]{2,1,0:T(8,128)S(1)}, f32[32,6,64]{2,1,0:T(8,128)S(1)}) fusion(f32[32,4,6,64]{3,1,2,0:T(4,128)S(1)} %get-tuple-element.62, f32[32,4,6,64]{3,1,2,0:T(4,128)S(1)} %fusion.45, f32[32]{0:T(128)} %get-tuple-element.40, f32[32,6]{1,0:T(8,128)} %bitcast.79, f32[6]{0:T(128)} %param.30, f32[32,4,6,64]{3,1,2,0:T(4,128)S(1)} %get-tuple-element.61, ...), kind=kLoop, calls=%fused_computation.79 | loop fusion | flops 196608 | bytes 495640 | tf_op jit(solution)/shard_map/add | solution.py:175
  149.9 2.4 %fusion.31 = (f32[32,6,64]{2,1,0:T(8,128)S(1)}, f32[32,6,64]{2,1,0:T(8,128)S(1)}) fusion(f32[32,4,6,64]{3,1,2,0:T(4,128)S(1)} %get-tuple-element.62, f32[32,4,6,64]{3,1,2,0:T(4,128)S(1)} %fusion.45, f32[32]{0:T(128)} %get-tuple-element.48, f32[32,6]{1,0:T(8,128)S(1)} %copy.244, f32[32,6]{1,0:T(8,128)S(1)} %copy.243, f32[6]{0:T(128)} %param.30, ...), kind=kLoop, calls=%fused_computation.78 | loop fusion | flops 196608 | bytes 446488 | tf_op jit(solution)/shard_map/add | solution.py:175
  157.5 13.4 %add_convert_fusion = bf16[32,6,64,128]{3,2,1,0:T(8,128)(2,1)} fusion(bf16[32,6,64,128]{3,2,1,0:T(8,128)(2,1)} %bitcast.71, f32[32,6]{1,0:T(8,128)S(1)} %copy-done.10, f32[32,4,6,64]{3,1,2,0:T(4,128)S(1)} %get-tuple-element.61, f32[32,4,6]{1,2,0:T(8,128)S(1)} %copy.259, f32[32,4,256]{2,1,0:T(4,128)S(1)} %divide_multiply_fusion.1), kind=kOutput, calls=%fused_computation.6 | convolution fusion | flops 81838080 | bytes 6897664 | tf_op jit(solution)/shard_map/rshp,rsn->rhpn/dot_general | solution.py:179
  170.9 19.9 %reduce-scatter.2.cloned.1.call-done = f32[16,1664]{1,0:T(8,128)} async-done(((f32[128,1664]{1,0:T(8,128)}), f32[16,1664]{1,0:T(8,128)}) %reduce-scatter.2.cloned.1.call-update) | async-done | bytes 106512 | tf_op jit(solution)/shard_map/reduce_scatter | solution.py:193
  191.6 1.6 fusion.18
  (155 shorter events, 33.7 us)
Async XLA Ops:
  7.2 146.8 %copy-start = (bf16[384,1536]{1,0:T(8,128)(2,1)S(1)}, bf16[384,1536]{1,0:T(8,128)(2,1)}, u32[]{:S(2)}) copy-start(bf16[384,1536]{1,0:T(8,128)(2,1)} %param.32) | copy-start | bytes 3538948
  11.1 14.4 %copy-start.8 = (bf16[16,1536]{1,0:T(8,128)(2,1)S(1)}, bf16[16,1536]{1,0:T(8,128)(2,1)}, u32[]{:S(2)}) copy-start(bf16[16,1536]{1,0:T(8,128)(2,1)} %param.20) | copy-start | bytes 147460
  11.1 14.6 %copy-start.18 = (s32[1024]{0:T(1024)S(1)}, s32[1024]{0:T(1024)}, u32[]{:S(2)}) copy-start(s32[1024]{0:T(1024)} %param.39) | copy-start | bytes 12292
  11.1 19.9 %copy-start.27 = (s32[32]{0:T(128)S(1)}, s32[32]{0:T(128)}, u32[]{:S(2)}) copy-start(s32[32]{0:T(128)} %param.38) | copy-start | bytes 388
  13.4 1.7 copy-start.1
  15.1 26.4 %copy-start.16 = (f32[1536]{0:T(1024)S(1)}, f32[1536]{0:T(1024)}, u32[]{:S(2)}) copy-start(f32[1536]{0:T(1024)} %param.21) | copy-start | bytes 18436
  17.9 13.9 %all-to-all-start.1 = ((bf16[32,2,798]{2,1,0:T(2,128)(2,1)}), bf16[32,2,798]{2,1,0:T(2,128)(2,1)S(1)}, u32[]{:S(2)}, u32[]{:S(2)}) async-start(bf16[32,2,798]{2,1,0:T(2,128)(2,1)} %reshape.429), calls=%async_computation.1 | async-start | bytes 229376 | tf_op jit(solution)/shard_map/all_to_all | solution.py:50
  34.2 13.3 %all-to-all-start.2 = ((bf16[32,2,798]{2,1,0:T(2,128)(2,1)}), bf16[32,2,798]{2,1,0:T(2,128)(2,1)S(1)}, u32[]{:S(2)}, u32[]{:S(2)}) async-start(bf16[32,2,798]{2,1,0:T(2,128)(2,1)} %reshape.431), calls=%async_computation.2 | async-start | bytes 229376 | tf_op jit(solution)/shard_map/all_to_all | solution.py:53
  48.3 23.4 %all-to-all-start = ((bf16[8,16,1536]{2,1,0:T(8,128)(2,1)}), bf16[8,16,1536]{2,1,0:T(8,128)(2,1)S(1)}, u32[]{:S(2)}, u32[]{:S(2)}) async-start(bf16[8,16,1536]{2,1,0:T(8,128)(2,1)} %stack.14), calls=%async_computation | async-start | bytes 786432 | tf_op jit(solution)/shard_map/all_to_all | solution.py:95
  71.7 0.7 copy-start.3
  72.4 45.8 %all-to-all-start.3 = ((bf16[32,399,128]{2,1,0:T(8,128)(2,1)}), bf16[32,399,128]{2,1,0:T(8,128)(2,1)}, u32[]{:S(2)}, u32[]{:S(2)}) async-start(bf16[32,399,128]{2,1,0:T(8,128)(2,1)} %broadcast_select_fusion), calls=%async_computation.3 | async-start | bytes 6553600 | tf_op jit(solution)/shard_map/all_to_all | solution.py:129
  78.9 3.4 %copy-start.17 = (f32[4,384]{1,0:T(4,128)S(1)}, f32[4,384]{1,0:T(4,128)}, u32[]{:S(2)}) copy-start(f32[4,384]{1,0:T(4,128)} %param.24) | copy-start | bytes 18436
  78.9 111.9 %reduce-scatter.2.cloned.1.call-start = ((), (), s32[]{:S(2)}) async-start(), calls=%async_computation.5 | async-start | bytes 958464 | tf_op jit(solution)/shard_map/reduce_scatter | solution.py:193
  83.5 39.5 %copy-start.24 = (pred[32,4]{0,1:T(4,128)(4,1)}, pred[32,4]{0,1:T(4,128)(4,1)S(1)}, u32[]{:S(2)}) copy-start(pred[32,4]{0,1:T(4,128)(4,1)S(1)} %iota_compare_fusion.1) | copy-start | bytes 388
  123.0 4.1 %copy-start.2 = (bf16[32,399,128]{2,1,0:T(8,128)(2,1)S(1)}, bf16[32,399,128]{2,1,0:T(8,128)(2,1)}, u32[]{:S(2)}) copy-start(bf16[32,399,128]{2,1,0:T(8,128)(2,1)} %gather_fusion.2) | copy-start | bytes 9805828
  123.0 4.2 %slice-start = ((bf16[32,399,128]{2,1,0:T(8,128)(2,1)}), bf16[32,9,128]{2,1,0:T(8,128)(2,1)S(1)}, s32[]{:S(2)}) async-start(bf16[32,399,128]{2,1,0:T(8,128)(2,1)} %gather_fusion.2), calls=%async_computation.6 | async-start | bytes 262144 | tf_op jit(solution)/shard_map/slice | solution.py:132
  123.0 4.3 %copy-start.13 = (f32[384]{0:T(512)S(1)}, f32[384]{0:T(512)}, u32[]{:S(2)}) copy-start(f32[384]{0:T(512)} %get-tuple-element.51) | copy-start | bytes 4612
  123.0 4.3 %copy-start.14 = (f32[384]{0:T(512)S(1)}, f32[384]{0:T(512)}, u32[]{:S(2)}) copy-start(f32[384]{0:T(512)} %get-tuple-element.52) | copy-start | bytes 4612
  123.0 4.3 %copy-start.15 = (f32[384]{0:T(512)S(1)}, f32[384]{0:T(512)}, u32[]{:S(2)}) copy-start(f32[384]{0:T(512)} %get-tuple-element.53) | copy-start | bytes 4612
  123.0 4.3 %copy-start.23 = (f32[384]{0:T(512)S(1)}, f32[384]{0:T(512)}, u32[]{:S(2)}) copy-start(f32[384]{0:T(512)} %param.25) | copy-start | bytes 4612
  123.0 4.6 %copy-start.5 = (bf16[32,4,256]{2,1,0:T(4,128)(2,1)S(1)}, bf16[32,4,256]{2,1,0:T(4,128)(2,1)}, u32[]{:S(2)}) copy-start(bf16[32,4,256]{2,1,0:T(4,128)(2,1)} %slice.269) | copy-start | bytes 196612
  127.1 0.7 copy-start.20
  127.1 0.7 copy-start.21
  127.1 0.7 copy-start.25
  127.6 14.2 %copy-start.6 = (bf16[32,3,256]{2,1,0:T(4,128)(2,1)}, bf16[32,3,256]{2,1,0:T(4,128)(2,1)S(1)}, u32[]{:S(2)}) copy-start(bf16[32,3,256]{2,1,0:T(4,128)(2,1)S(1)} %reshape.339) | copy-start | bytes 147460
  152.3 3.3 %copy-start.26 = (s32[32]{0:T(128)S(1)}, s32[32]{0:T(128)}, u32[]{:S(2)}) copy-start(s32[32]{0:T(128)} %param.36) | copy-start | bytes 388
  152.3 3.3 %copy-start.11 = (f32[32,1,6]{0,1,2:T(1,128)S(1)}, f32[32,1,6]{0,1,2:T(1,128)}, u32[]{:S(2)}) copy-start(f32[32,1,6]{0,1,2:T(1,128)} %get-tuple-element.54) | copy-start | bytes 2308
  152.3 3.2 %copy-start.12 = (f32[32,1,6]{0,1,2:T(1,128)S(1)}, f32[32,1,6]{0,1,2:T(1,128)}, u32[]{:S(2)}) copy-start(f32[32,1,6]{0,1,2:T(1,128)} %get-tuple-element.55) | copy-start | bytes 2308
  152.5 3.3 %copy-start.4 = (bf16[32,4,304]{2,1,0:T(4,128)(2,1)S(1)}, bf16[32,4,304]{2,1,0:T(4,128)(2,1)}, u32[]{:S(2)}) copy-start(bf16[32,4,304]{2,1,0:T(4,128)(2,1)} %reshape.335) | copy-start | bytes 233476
  152.5 3.3 %copy-start.7 = (bf16[32,3,256]{2,1,0:T(4,128)(2,1)S(1)}, bf16[32,3,256]{2,1,0:T(4,128)(2,1)}, u32[]{:S(2)}) copy-start(bf16[32,3,256]{2,1,0:T(4,128)(2,1)} %copy-done.6) | copy-start | bytes 147460
  153.9 3.6 %copy-start.10 = (f32[32,6]{1,0:T(8,128)S(1)}, f32[32,6]{1,0:T(8,128)}, u32[]{:S(2)}) copy-start(f32[32,6]{1,0:T(8,128)} %copy.250) | copy-start | bytes 2308
  157.5 34.1 %copy-start.9 = (bf16[16,1536]{1,0:T(8,128)(2,1)S(1)}, bf16[16,1536]{1,0:T(8,128)(2,1)}, u32[]{:S(2)}) copy-start(bf16[16,1536]{1,0:T(8,128)(2,1)} %param.20) | copy-start | bytes 147460
  (2 other events, 1.3 us)
Sparse Core Ops, SparseCore 0:
  155.6 35.1 reduce-scatter.1
